TPU v7x, 32 devices: a whole 2x2x4 slice. The times are simulated.
32 devices in a mesh: gx: 8 (over y, x, core), gy: 4 (over z).
Axes of the slice: x: 2, y: 2, z: 4, core: 2. Of those that a mesh axis runs over, the one named last changes fastest.
Arguments:
- forcing: float32 [64, 64, 512], P('gx', 'gy'), may hold values from -5 to 5
- coefficient: float32 [64, 64, 512], P('gx', 'gy'), may hold values from 0.5 to 2
- guess: float32 [64, 64, 512], P('gx', 'gy'), may hold values from -3 to 3
Outputs:
- pressure: float32 [64, 64, 512], P('gx', 'gy')
- residual: float32 [64, 64, 512], P('gx', 'gy')
All inputs are finite; a program needn't handle non-finite values.
Results may differ from a plain program's by a relative error of at most 0.000028.
Values sent between devices are 32-bit elements; how exact they have to be, the bound alone decides.
A program may use at most 64 MiB of HBM per device.

v0:
```python
import jax
import jax.numpy as jnp
from jax import lax
from jax.sharding import PartitionSpec as P

CPRE = 3
CPOST = 2
CCOARSE = 4


theta = 1.15
delta = 0.85


def extended(cells, sides, width):
    for axis, dim in sides:
        count = lax.axis_size(axis)
        ends = count - 1
        head = lax.slice_in_dim(cells, 0, width, axis=dim)
        tail = lax.slice_in_dim(cells, cells.shape[dim] - width, cells.shape[dim], axis=dim)
        cells = jnp.concatenate(
            [
                lax.ppermute(tail, axis, [(i, (i + 1) % count) for i in range(ends)]),
                cells,
                lax.ppermute(head, axis, [((i + 1) % count, i) for i in range(ends)]),
            ],
            axis=dim,
        )
    return cells


def laplace(padded):
    center = padded[1:-1, 1:-1, 1:-1]
    beside = padded[2:, 1:-1, 1:-1] + padded[:-2, 1:-1, 1:-1]
    beside = beside + padded[1:-1, 2:, 1:-1] + padded[1:-1, :-2, 1:-1]
    beside = beside + padded[1:-1, 1:-1, 2:] + padded[1:-1, 1:-1, :-2]
    return 6.0 * center - beside


def chebyshev(state, remain, passes, operator, inverse):
    sigma = theta / delta
    rho = 1.0 / sigma
    direction = inverse * remain / theta
    for step in range(passes):
        if step > 0:
            rho_next = 1.0 / (2.0 * sigma - rho)
            direction = rho_next * rho * direction + 2.0 * rho_next / delta * (inverse * remain)
            rho = rho_next
        state = state + direction
        remain = remain - operator(direction)
    return (state, remain)


def inside_mask(rows, cols, depth):
    glob_x = lax.axis_index("gx") * rows - depth + jnp.arange(rows + 2 * depth)
    glob_y = lax.axis_index("gy") * cols - depth + jnp.arange(cols + 2 * depth)
    mask_x = ((glob_x >= 0) & (glob_x < rows * lax.axis_size("gx"))).astype(jnp.float32)
    mask_y = ((glob_y >= 0) & (glob_y < cols * lax.axis_size("gy"))).astype(jnp.float32)
    return (mask_x[:, None] * mask_y[None, :])[:, :, None]


def fine_margin_section(state, forcing, coefficient, passes):
    depth = passes + 1
    rows, cols = (state.shape[0], state.shape[1])
    stacked = jnp.stack((state, forcing, coefficient))
    grown = extended(stacked, (("gx", 1), ("gy", 2)), depth)
    mask = inside_mask(rows, cols, depth)
    state_ext = grown[0]
    forcing_ext = grown[1]
    coef_ext = jnp.where(mask > 0.0, grown[2], 1.0)
    inverse = 1.0 / (6.0 * coef_ext * coef_ext)

    def local_op(value):
        return mask * (coef_ext * laplace(jnp.pad(coef_ext * value, 1)))

    remain = forcing_ext - local_op(state_ext)
    state_ext, remain = chebyshev(state_ext, remain, passes, local_op, inverse)
    return (
        state_ext[depth : depth + rows, depth : depth + cols],
        remain[depth : depth + rows, depth : depth + cols],
    )


def fine_section(state, forcing, coefficient, passes):
    return fine_margin_section(state, forcing, coefficient, passes)


def per_device(forcing, coefficient, guess):
    state, remain = fine_section(guess, forcing, coefficient, CPRE)
    sx, sy, sz = remain.shape
    coarse_rhs = remain.reshape(sx // 2, 2, sy // 2, 2, sz // 2, 2).sum(axis=(1, 3, 5))
    coarse_coef = coefficient.reshape(sx // 2, 2, sy // 2, 2, sz // 2, 2).sum(axis=(1, 3, 5)) / 8.0
    coarse_inverse = 1.0 / (24.0 * coarse_coef * coarse_coef)

    def coarse_op(value):
        padded = extended(coarse_coef * value, (("gx", 0), ("gy", 1)), 1)
        padded = jnp.pad(padded, ((0, 0), (0, 0), (1, 1)))
        return 4.0 * coarse_coef * laplace(padded)

    correction, unused = chebyshev(
        jnp.zeros_like(coarse_rhs), coarse_rhs, CCOARSE, coarse_op, coarse_inverse
    )
    fine_corr = jnp.repeat(jnp.repeat(jnp.repeat(correction, 2, axis=0), 2, axis=1), 2, axis=2)
    state = state + fine_corr
    state, remain = fine_section(state, forcing, coefficient, CPOST)
    return (state, remain)


def solution(mesh):
    return jax.shard_map(
        per_device,
        mesh=mesh,
        in_specs=(P("gx", "gy", None), P("gx", "gy", None), P("gx", "gy", None)),
        out_specs=(P("gx", "gy", None), P("gx", "gy", None)),
        check_vma=False,
    )
```

profile of v0, /device:TPU:1, one launch (start us, length us, event | category | flops | bytes accessed | tf_op | source)
XLA Modules:
  0.0 156.7 jit_solution(8915590200069098427)
XLA Ops:
  1.9 4.5 %collective-permute-start = (f32[3,4,16,512]{3,2,1,0:T(8,128)S(1)}, f32[3,4,16,512]{3,2,1,0:T(8,128)S(1)}, u32[]{:S(2)}, u32[]{:S(2)}) collective-permute-start(f32[3,4,16,512]{3,2,1,0:T(8,128)S(1)} %get-tuple-element.36), channel_id=1, source_target_pairs={{0,4},{4,8},{8,12},{12,16},{16,20},{20,24},{24,28},{1,5},{5,9},{9,... | collective-permute-start | bytes 1179656 | tf_op jit(solution)/shard_map/ppermute | solution.py:23
  6.4 1.9 %collective-permute-start.1 = (f32[3,4,16,512]{3,2,1,0:T(8,128)S(1)}, f32[3,4,16,512]{3,2,1,0:T(8,128)S(1)}, u32[]{:S(2)}, u32[]{:S(2)}) collective-permute-start(f32[3,4,16,512]{3,2,1,0:T(8,128)S(1)} %get-tuple-element.37), channel_id=1, source_target_pairs={{4,0},{8,4},{12,8},{16,12},{20,16},{24,20},{28,24},{5,1},{9,5},{13... | collective-permute-start | bytes 1179656 | tf_op jit(solution)/shard_map/ppermute | solution.py:25
  8.4 18.1 %reshape.161 = f32[4,2,8,2,256,2]{5,4,3,2,1,0:T(8,128)} reshape(f32[8,16,512]{2,1,0:T(8,128)S(1)} %copy-done) | data formatting | bytes 524288 | tf_op jit(solution)/shard_map/reshape | solution.py:92
  28.3 4.0 %collective-permute-start.2 = (f32[3,16,4,512]{3,1,2,0:T(8,128)S(1)}, f32[3,16,4,512]{3,1,2,0:T(8,128)S(1)}, u32[]{:S(2)}, u32[]{:S(2)}) collective-permute-start(f32[3,16,4,512]{3,1,2,0:T(8,128)S(1)} %copy.57), channel_id=1, source_target_pairs={{0,1},{1,2},{2,3},{4,5},{5,6},{6,7},{8,9},{9,10},{10,11},{12,13},{... | collective-permute-start | bytes 1179656 | tf_op jit(solution)/shard_map/ppermute | solution.py:23
  32.5 7.6 %reduce_sum.18 = f32[4,8,256]{2,1,0:T(8,128)} reduce(f32[4,2,8,2,256,2]{5,4,3,2,1,0:T(8,128)} %reshape.161, f32[]{:T(128)} %constant.31.clone.1), dimensions={1,3,5}, to_apply=%region_0.1 | reduce | flops 57344 | bytes 294916 | tf_op jit(solution)/shard_map/reduce_sum | solution.py:92
  42.3 1.7 %broadcast_multiply_fusion = (f32[16,24,512]{2,1,0:T(8,128)}, f32[16,24,512]{2,1,0:T(8,128)S(1)}) fusion(f32[16,24,512]{2,1,0:T(8,128)S(1)} %get-tuple-element.26, f32[16,24,512]{2,1,0:T(8,128)S(1)} %get-tuple-element.25, f32[16,24]{1,0:T(8,128)S(1)} %broadcast_multiply_fusion.3, f32[3,16,24,512]{3,2,1,0:T(8,128)S(1)} %pad_maximum_fusion), kind=kLoop, calls=%fused_computation.119 | loop fusion | flops 2949120 | bytes 3933696 | tf_op jit(solution)/shard_map/div | solution.py:43
  45.1 1.8 %fusion.95 = (f32[16,24,512]{2,1,0:T(8,128)S(1)}, f32[16,24,512]{2,1,0:T(8,128)}, f32[16,24,512]{2,1,0:T(8,128)S(1)}) fusion(f32[16,24,512]{2,1,0:T(8,128)S(1)} %get-tuple-element.26, f32[16,24,512]{2,1,0:T(8,128)S(1)} %get-tuple-element.23, f32[16,24,512]{2,1,0:T(8,128)S(1)} %get-tuple-element.24, f32[16,24,512]{2,1,0:T(8,128)S(1)} %get-tuple-element.22, ...), kind=kLoop, calls=%fused_computation.242 | loop fusion | flops 3538944 | bytes 5506560 | tf_op jit(solution)/shard_map/mul | solution.py:74
  47.7 18.1 %reshape.162 = f32[4,2,8,2,256,2]{5,4,3,2,1,0:T(8,128)} reshape(f32[8,16,512]{2,1,0:T(8,128)S(1)} %slice_subtract_fusion.1) | data formatting | bytes 524288 | tf_op jit(solution)/shard_map/reshape | solution.py:91
  65.8 7.0 %reduce_sum.19 = f32[4,8,256]{2,1,0:T(8,128)S(1)} reduce(f32[4,2,8,2,256,2]{5,4,3,2,1,0:T(8,128)} %reshape.162, f32[]{:T(128)} %constant.31.clone.1), dimensions={1,3,5}, to_apply=%region_1.2 | reduce | flops 57344 | bytes 294916 | tf_op jit(solution)/shard_map/reduce_sum | solution.py:91
  72.8 4.2 %collective-permute-start.5 = (f32[1,8,256]{2,1,0:T(8,128)S(1)}, f32[1,8,256]{2,1,0:T(8,128)S(1)}, u32[]{:S(2)}, u32[]{:S(2)}) collective-permute-start(f32[1,8,256]{2,1,0:T(8,128)S(1)} %get-tuple-element.51), channel_id=1, source_target_pairs={{0,4},{4,8},{8,12},{12,16},{16,20},{20,24},{24,28},{1,5},{5,9},{9,... | collective-permute-start | bytes 24584 | tf_op jit(solution)/shard_map/ppermute | solution.py:23
  77.0 1.9 %collective-permute-start.4 = (f32[1,8,256]{2,1,0:T(8,128)S(1)}, f32[1,8,256]{2,1,0:T(8,128)S(1)}, u32[]{:S(2)}, u32[]{:S(2)}) collective-permute-start(f32[1,8,256]{2,1,0:T(8,128)S(1)} %get-tuple-element.52), channel_id=1, source_target_pairs={{4,0},{8,4},{12,8},{16,12},{20,16},{24,20},{28,24},{5,1},{9,5},{13... | collective-permute-start | bytes 24584 | tf_op jit(solution)/shard_map/ppermute | solution.py:25
  78.9 3.0 %collective-permute-done.4 = f32[1,8,256]{2,1,0:T(8,128)S(1)} collective-permute-done((f32[1,8,256]{2,1,0:T(8,128)S(1)}, f32[1,8,256]{2,1,0:T(8,128)S(1)}, u32[]{:S(2)}, u32[]{:S(2)}) %collective-permute-start.4) | collective-permute-done | bytes 8224 | tf_op jit(solution)/shard_map/ppermute | solution.py:25
  82.0 4.1 %collective-permute-start.7 = (f32[6,1,256]{2,1,0:T(1,128)S(1)}, f32[6,1,256]{2,1,0:T(1,128)S(1)}, u32[]{:S(2)}, u32[]{:S(2)}) collective-permute-start(f32[6,1,256]{2,1,0:T(1,128)S(1)} %get-tuple-element.45), channel_id=1, source_target_pairs={{0,1},{1,2},{2,3},{4,5},{5,6},{6,7},{8,9},{9,10},{10,11},{12,13},{... | collective-permute-start | bytes 18440 | tf_op jit(solution)/shard_map/ppermute | solution.py:23
  87.4 3.1 %collective-permute-done.6 = f32[6,1,256]{2,1,0:T(1,128)S(1)} collective-permute-done((f32[6,1,256]{2,1,0:T(1,128)S(1)}, f32[6,1,256]{2,1,0:T(1,128)S(1)}, u32[]{:S(2)}, u32[]{:S(2)}) %collective-permute-start.6) | collective-permute-done | bytes 6176 | tf_op jit(solution)/shard_map/ppermute | solution.py:25
  90.7 3.4 %collective-permute-start.9 = (f32[1,8,256]{2,1,0:T(8,128)S(1)}, f32[1,8,256]{2,1,0:T(8,128)S(1)}, u32[]{:S(2)}, u32[]{:S(2)}) collective-permute-start(f32[1,8,256]{2,1,0:T(8,128)S(1)} %get-tuple-element.49), channel_id=1, source_target_pairs={{0,4},{4,8},{8,12},{12,16},{16,20},{20,24},{24,28},{1,5},{5,9},{9,... | collective-permute-start | bytes 24584 | tf_op jit(solution)/shard_map/ppermute | solution.py:23
  94.1 1.9 %collective-permute-start.8 = (f32[1,8,256]{2,1,0:T(8,128)S(1)}, f32[1,8,256]{2,1,0:T(8,128)S(1)}, u32[]{:S(2)}, u32[]{:S(2)}) collective-permute-start(f32[1,8,256]{2,1,0:T(8,128)S(1)} %get-tuple-element.50), channel_id=1, source_target_pairs={{4,0},{8,4},{12,8},{16,12},{20,16},{24,20},{28,24},{5,1},{9,5},{13... | collective-permute-start | bytes 24584 | tf_op jit(solution)/shard_map/ppermute | solution.py:25
  96.0 3.0 %collective-permute-done.8 = f32[1,8,256]{2,1,0:T(8,128)S(1)} collective-permute-done((f32[1,8,256]{2,1,0:T(8,128)S(1)}, f32[1,8,256]{2,1,0:T(8,128)S(1)}, u32[]{:S(2)}, u32[]{:S(2)}) %collective-permute-start.8) | collective-permute-done | bytes 8224 | tf_op jit(solution)/shard_map/ppermute | solution.py:25
  99.1 3.2 %collective-permute-start.11 = (f32[6,1,256]{2,1,0:T(1,128)S(1)}, f32[6,1,256]{2,1,0:T(1,128)S(1)}, u32[]{:S(2)}, u32[]{:S(2)}) collective-permute-start(f32[6,1,256]{2,1,0:T(1,128)S(1)} %get-tuple-element.43), channel_id=1, source_target_pairs={{0,1},{1,2},{2,3},{4,5},{5,6},{6,7},{8,9},{9,10},{10,11},{12,13},{... | collective-permute-start | bytes 18440 | tf_op jit(solution)/shard_map/ppermute | solution.py:23
  103.6 3.1 %collective-permute-done.10 = f32[6,1,256]{2,1,0:T(1,128)S(1)} collective-permute-done((f32[6,1,256]{2,1,0:T(1,128)S(1)}, f32[6,1,256]{2,1,0:T(1,128)S(1)}, u32[]{:S(2)}, u32[]{:S(2)}) %collective-permute-start.10) | collective-permute-done | bytes 6176 | tf_op jit(solution)/shard_map/ppermute | solution.py:25
  106.9 3.4 %collective-permute-start.13 = (f32[1,8,256]{2,1,0:T(8,128)S(1)}, f32[1,8,256]{2,1,0:T(8,128)S(1)}, u32[]{:S(2)}, u32[]{:S(2)}) collective-permute-start(f32[1,8,256]{2,1,0:T(8,128)S(1)} %get-tuple-element.47), channel_id=1, source_target_pairs={{0,4},{4,8},{8,12},{12,16},{16,20},{20,24},{24,28},{1,5},{5,9},{9,... | collective-permute-start | bytes 24584 | tf_op jit(solution)/shard_map/ppermute | solution.py:23
  110.4 1.9 %collective-permute-start.12 = (f32[1,8,256]{2,1,0:T(8,128)S(1)}, f32[1,8,256]{2,1,0:T(8,128)S(1)}, u32[]{:S(2)}, u32[]{:S(2)}) collective-permute-start(f32[1,8,256]{2,1,0:T(8,128)S(1)} %get-tuple-element.48), channel_id=1, source_target_pairs={{4,0},{8,4},{12,8},{16,12},{20,16},{24,20},{28,24},{5,1},{9,5},{13... | collective-permute-start | bytes 24584 | tf_op jit(solution)/shard_map/ppermute | solution.py:25
  112.3 3.2 %collective-permute-done.12 = f32[1,8,256]{2,1,0:T(8,128)S(1)} collective-permute-done((f32[1,8,256]{2,1,0:T(8,128)S(1)}, f32[1,8,256]{2,1,0:T(8,128)S(1)}, u32[]{:S(2)}, u32[]{:S(2)}) %collective-permute-start.12) | collective-permute-done | bytes 8224 | tf_op jit(solution)/shard_map/ppermute | solution.py:25
  115.5 3.2 %collective-permute-start.15 = (f32[6,1,256]{2,1,0:T(1,128)S(1)}, f32[6,1,256]{2,1,0:T(1,128)S(1)}, u32[]{:S(2)}, u32[]{:S(2)}) collective-permute-start(f32[6,1,256]{2,1,0:T(1,128)S(1)} %get-tuple-element.41), channel_id=1, source_target_pairs={{0,1},{1,2},{2,3},{4,5},{5,6},{6,7},{8,9},{9,10},{10,11},{12,13},{... | collective-permute-start | bytes 18440 | tf_op jit(solution)/shard_map/ppermute | solution.py:23
  118.7 1.5 collective-permute-start.14
  121.1 2.0 %collective-permute-done.14 = f32[6,1,256]{2,1,0:T(1,128)S(1)} collective-permute-done((f32[6,1,256]{2,1,0:T(1,128)S(1)}, f32[6,1,256]{2,1,0:T(1,128)S(1)}, u32[]{:S(2)}, u32[]{:S(2)}) %collective-permute-start.14) | collective-permute-done | bytes 6176 | tf_op jit(solution)/shard_map/ppermute | solution.py:25
  126.9 1.6 %fusion.60 = f32[1,8,16,512]{3,2,1,0:T(8,128)S(1)} fusion(f32[8,16,512]{2,1,0:T(8,128)S(1)} %copy.52, f32[16,24,512]{2,1,0:T(8,128)} %get-tuple-element.20, f32[16,24,512]{2,1,0:T(8,128)} %copy-done.2, f32[16,24,512]{2,1,0:T(8,128)} %get-tuple-element.13, f32[16,24,512]{2,1,0:T(8,128)} %slice_bitcast_fusion.2), kind=kLoop, calls=%fused_computation.144 | loop fusion | flops 262144 | bytes 1572864 | tf_op jit(solution)/shard_map/stack | solution.py:65
  128.6 4.1 %collective-permute-start.16 = (f32[3,3,16,512]{3,2,1,0:T(8,128)S(1)}, f32[3,3,16,512]{3,2,1,0:T(8,128)S(1)}, u32[]{:S(2)}, u32[]{:S(2)}) collective-permute-start(f32[3,3,16,512]{3,2,1,0:T(8,128)S(1)} %get-tuple-element.31), channel_id=1, source_target_pairs={{0,4},{4,8},{8,12},{12,16},{16,20},{20,24},{24,28},{1,5},{5,9},{9,... | collective-permute-start | bytes 884744 | tf_op jit(solution)/shard_map/ppermute | solution.py:23
  132.7 1.9 %collective-permute-start.17 = (f32[3,3,16,512]{3,2,1,0:T(8,128)S(1)}, f32[3,3,16,512]{3,2,1,0:T(8,128)S(1)}, u32[]{:S(2)}, u32[]{:S(2)}) collective-permute-start(f32[3,3,16,512]{3,2,1,0:T(8,128)S(1)} %get-tuple-element.32), channel_id=1, source_target_pairs={{4,0},{8,4},{12,8},{16,12},{20,16},{24,20},{28,24},{5,1},{9,5},{13... | collective-permute-start | bytes 884744 | tf_op jit(solution)/shard_map/ppermute | solution.py:25
  134.7 1.7 %collective-permute-done.16 = f32[3,3,16,512]{3,2,1,0:T(8,128)S(1)} collective-permute-done((f32[3,3,16,512]{3,2,1,0:T(8,128)S(1)}, f32[3,3,16,512]{3,2,1,0:T(8,128)S(1)}, u32[]{:S(2)}, u32[]{:S(2)}) %collective-permute-start.16) | collective-permute-done | bytes 294944 | tf_op jit(solution)/shard_map/ppermute | solution.py:23
  136.3 6.8 %collective-permute-done.17 = f32[3,3,16,512]{3,2,1,0:T(8,128)S(1)} collective-permute-done((f32[3,3,16,512]{3,2,1,0:T(8,128)S(1)}, f32[3,3,16,512]{3,2,1,0:T(8,128)S(1)}, u32[]{:S(2)}, u32[]{:S(2)}) %collective-permute-start.17) | collective-permute-done | bytes 294944 | tf_op jit(solution)/shard_map/ppermute | solution.py:25
  144.8 4.0 %collective-permute-start.18 = (f32[3,14,3,512]{3,1,2,0:T(8,128)S(1)}, f32[3,14,3,512]{3,1,2,0:T(8,128)S(1)}, u32[]{:S(2)}, u32[]{:S(2)}) collective-permute-start(f32[3,14,3,512]{3,1,2,0:T(8,128)S(1)} %copy.59), channel_id=1, source_target_pairs={{0,1},{1,2},{2,3},{4,5},{5,6},{6,7},{8,9},{9,10},{10,11},{12,13},{... | collective-permute-start | bytes 774152 | tf_op jit(solution)/shard_map/ppermute | solution.py:23
  149.1 1.9 %collective-permute-done.19 = f32[3,14,3,512]{3,1,2,0:T(8,128)S(1)} collective-permute-done((f32[3,14,3,512]{3,1,2,0:T(8,128)S(1)}, f32[3,14,3,512]{3,1,2,0:T(8,128)S(1)}, u32[]{:S(2)}, u32[]{:S(2)}) %collective-permute-start.19) | collective-permute-done | bytes 258080 | tf_op jit(solution)/shard_map/ppermute | solution.py:25
  (86 shorter events, 22.6 us)
Async XLA Ops:
  0.6 7.7 %copy-start = (f32[8,16,512]{2,1,0:T(8,128)S(1)}, f32[8,16,512]{2,1,0:T(8,128)}, u32[]{:S(2)}) copy-start(f32[8,16,512]{2,1,0:T(8,128)} %param.4) | copy-start | bytes 786436
  1.9 24.6 %collective-permute-start = (f32[3,4,16,512]{3,2,1,0:T(8,128)S(1)}, f32[3,4,16,512]{3,2,1,0:T(8,128)S(1)}, u32[]{:S(2)}, u32[]{:S(2)}) collective-permute-start(f32[3,4,16,512]{3,2,1,0:T(8,128)S(1)} %get-tuple-element.36), channel_id=1, source_target_pairs={{0,4},{4,8},{8,12},{12,16},{16,20},{20,24},{24,28},{1,5},{5,9},{9,... | collective-permute-start | bytes 1179656 | tf_op jit(solution)/shard_map/ppermute | solution.py:23
  6.4 20.1 %collective-permute-start.1 = (f32[3,4,16,512]{3,2,1,0:T(8,128)S(1)}, f32[3,4,16,512]{3,2,1,0:T(8,128)S(1)}, u32[]{:S(2)}, u32[]{:S(2)}) collective-permute-start(f32[3,4,16,512]{3,2,1,0:T(8,128)S(1)} %get-tuple-element.37), channel_id=1, source_target_pairs={{4,0},{8,4},{12,8},{16,12},{20,16},{24,20},{28,24},{5,1},{9,5},{13... | collective-permute-start | bytes 1179656 | tf_op jit(solution)/shard_map/ppermute | solution.py:25
  8.4 18.1 %copy-start.1 = (f32[8,16,512]{2,1,0:T(8,128)S(1)}, f32[8,16,512]{2,1,0:T(8,128)}, u32[]{:S(2)}) copy-start(f32[8,16,512]{2,1,0:T(8,128)} %param.3) | copy-start | bytes 786436
  8.4 18.1 %copy-start.3 = (f32[8,16,512]{2,1,0:T(8,128)S(1)}, f32[8,16,512]{2,1,0:T(8,128)}, u32[]{:S(2)}) copy-start(f32[8,16,512]{2,1,0:T(8,128)} %param.5) | copy-start | bytes 786436
  26.5 13.5 %copy-start.4 = (f32[3,4,16,512]{3,2,1,0:T(8,128)}, f32[3,4,16,512]{3,2,1,0:T(8,128)S(1)}, u32[]{:S(2)}) copy-start(f32[3,4,16,512]{3,2,1,0:T(8,128)S(1)} %collective-permute-done.1) | copy-start | bytes 1179652
  27.0 13.1 %collective-permute-start.3 = (f32[3,16,4,512]{3,1,2,0:T(8,128)S(1)}, f32[3,16,4,512]{3,1,2,0:T(8,128)S(1)}, u32[]{:S(2)}, u32[]{:S(2)}) collective-permute-start(f32[3,16,4,512]{3,1,2,0:T(8,128)S(1)} %copy.58), channel_id=1, source_target_pairs={{1,0},{2,1},{3,2},{5,4},{6,5},{7,6},{9,8},{10,9},{11,10},{13,12},{... | collective-permute-start | bytes 1179656 | tf_op jit(solution)/shard_map/ppermute | solution.py:25
  28.3 12.1 %collective-permute-start.2 = (f32[3,16,4,512]{3,1,2,0:T(8,128)S(1)}, f32[3,16,4,512]{3,1,2,0:T(8,128)S(1)}, u32[]{:S(2)}, u32[]{:S(2)}) collective-permute-start(f32[3,16,4,512]{3,1,2,0:T(8,128)S(1)} %copy.57), channel_id=1, source_target_pairs={{0,1},{1,2},{2,3},{4,5},{5,6},{6,7},{8,9},{9,10},{10,11},{12,13},{... | collective-permute-start | bytes 1179656 | tf_op jit(solution)/shard_map/ppermute | solution.py:23
  45.1 1.8 %copy-start.2 = (f32[16,24,512]{2,1,0:T(8,128)}, f32[16,24,512]{2,1,0:T(8,128)S(1)}, u32[]{:S(2)}) copy-start(f32[16,24,512]{2,1,0:T(8,128)S(1)} %get-tuple-element.23) | copy-start | bytes 2359300
  65.8 7.0 %copy-start.5 = (f32[4,8,256]{2,1,0:T(8,128)S(1)}, f32[4,8,256]{2,1,0:T(8,128)}, u32[]{:S(2)}) copy-start(f32[4,8,256]{2,1,0:T(8,128)} %reduce_sum.18) | copy-start | bytes 98308
  72.8 6.1 %collective-permute-start.5 = (f32[1,8,256]{2,1,0:T(8,128)S(1)}, f32[1,8,256]{2,1,0:T(8,128)S(1)}, u32[]{:S(2)}, u32[]{:S(2)}) collective-permute-start(f32[1,8,256]{2,1,0:T(8,128)S(1)} %get-tuple-element.51), channel_id=1, source_target_pairs={{0,4},{4,8},{8,12},{12,16},{16,20},{20,24},{24,28},{1,5},{5,9},{9,... | collective-permute-start | bytes 24584 | tf_op jit(solution)/shard_map/ppermute | solution.py:23
  77.0 5.0 %collective-permute-start.4 = (f32[1,8,256]{2,1,0:T(8,128)S(1)}, f32[1,8,256]{2,1,0:T(8,128)S(1)}, u32[]{:S(2)}, u32[]{:S(2)}) collective-permute-start(f32[1,8,256]{2,1,0:T(8,128)S(1)} %get-tuple-element.52), channel_id=1, source_target_pairs={{4,0},{8,4},{12,8},{16,12},{20,16},{24,20},{28,24},{5,1},{9,5},{13... | collective-permute-start | bytes 24584 | tf_op jit(solution)/shard_map/ppermute | solution.py:25
  82.0 5.4 %collective-permute-start.7 = (f32[6,1,256]{2,1,0:T(1,128)S(1)}, f32[6,1,256]{2,1,0:T(1,128)S(1)}, u32[]{:S(2)}, u32[]{:S(2)}) collective-permute-start(f32[6,1,256]{2,1,0:T(1,128)S(1)} %get-tuple-element.45), channel_id=1, source_target_pairs={{0,1},{1,2},{2,3},{4,5},{5,6},{6,7},{8,9},{9,10},{10,11},{12,13},{... | collective-permute-start | bytes 18440 | tf_op jit(solution)/shard_map/ppermute | solution.py:23
  86.1 4.4 %collective-permute-start.6 = (f32[6,1,256]{2,1,0:T(1,128)S(1)}, f32[6,1,256]{2,1,0:T(1,128)S(1)}, u32[]{:S(2)}, u32[]{:S(2)}) collective-permute-start(f32[6,1,256]{2,1,0:T(1,128)S(1)} %get-tuple-element.46), channel_id=1, source_target_pairs={{1,0},{2,1},{3,2},{5,4},{6,5},{7,6},{9,8},{10,9},{11,10},{13,12},{... | collective-permute-start | bytes 18440 | tf_op jit(solution)/shard_map/ppermute | solution.py:25
  90.7 5.3 %collective-permute-start.9 = (f32[1,8,256]{2,1,0:T(8,128)S(1)}, f32[1,8,256]{2,1,0:T(8,128)S(1)}, u32[]{:S(2)}, u32[]{:S(2)}) collective-permute-start(f32[1,8,256]{2,1,0:T(8,128)S(1)} %get-tuple-element.49), channel_id=1, source_target_pairs={{0,4},{4,8},{8,12},{12,16},{16,20},{20,24},{24,28},{1,5},{5,9},{9,... | collective-permute-start | bytes 24584 | tf_op jit(solution)/shard_map/ppermute | solution.py:23
  94.1 5.0 %collective-permute-start.8 = (f32[1,8,256]{2,1,0:T(8,128)S(1)}, f32[1,8,256]{2,1,0:T(8,128)S(1)}, u32[]{:S(2)}, u32[]{:S(2)}) collective-permute-start(f32[1,8,256]{2,1,0:T(8,128)S(1)} %get-tuple-element.50), channel_id=1, source_target_pairs={{4,0},{8,4},{12,8},{16,12},{20,16},{24,20},{28,24},{5,1},{9,5},{13... | collective-permute-start | bytes 24584 | tf_op jit(solution)/shard_map/ppermute | solution.py:25
  99.1 4.5 %collective-permute-start.11 = (f32[6,1,256]{2,1,0:T(1,128)S(1)}, f32[6,1,256]{2,1,0:T(1,128)S(1)}, u32[]{:S(2)}, u32[]{:S(2)}) collective-permute-start(f32[6,1,256]{2,1,0:T(1,128)S(1)} %get-tuple-element.43), channel_id=1, source_target_pairs={{0,1},{1,2},{2,3},{4,5},{5,6},{6,7},{8,9},{9,10},{10,11},{12,13},{... | collective-permute-start | bytes 18440 | tf_op jit(solution)/shard_map/ppermute | solution.py:23
  102.3 4.4 %collective-permute-start.10 = (f32[6,1,256]{2,1,0:T(1,128)S(1)}, f32[6,1,256]{2,1,0:T(1,128)S(1)}, u32[]{:S(2)}, u32[]{:S(2)}) collective-permute-start(f32[6,1,256]{2,1,0:T(1,128)S(1)} %get-tuple-element.44), channel_id=1, source_target_pairs={{1,0},{2,1},{3,2},{5,4},{6,5},{7,6},{9,8},{10,9},{11,10},{13,12},{... | collective-permute-start | bytes 18440 | tf_op jit(solution)/shard_map/ppermute | solution.py:25
  106.9 5.4 %collective-permute-start.13 = (f32[1,8,256]{2,1,0:T(8,128)S(1)}, f32[1,8,256]{2,1,0:T(8,128)S(1)}, u32[]{:S(2)}, u32[]{:S(2)}) collective-permute-start(f32[1,8,256]{2,1,0:T(8,128)S(1)} %get-tuple-element.47), channel_id=1, source_target_pairs={{0,4},{4,8},{8,12},{12,16},{16,20},{20,24},{24,28},{1,5},{5,9},{9,... | collective-permute-start | bytes 24584 | tf_op jit(solution)/shard_map/ppermute | solution.py:23
  110.4 5.1 %collective-permute-start.12 = (f32[1,8,256]{2,1,0:T(8,128)S(1)}, f32[1,8,256]{2,1,0:T(8,128)S(1)}, u32[]{:S(2)}, u32[]{:S(2)}) collective-permute-start(f32[1,8,256]{2,1,0:T(8,128)S(1)} %get-tuple-element.48), channel_id=1, source_target_pairs={{4,0},{8,4},{12,8},{16,12},{20,16},{24,20},{28,24},{5,1},{9,5},{13... | collective-permute-start | bytes 24584 | tf_op jit(solution)/shard_map/ppermute | solution.py:25
  115.5 5.6 %collective-permute-start.15 = (f32[6,1,256]{2,1,0:T(1,128)S(1)}, f32[6,1,256]{2,1,0:T(1,128)S(1)}, u32[]{:S(2)}, u32[]{:S(2)}) collective-permute-start(f32[6,1,256]{2,1,0:T(1,128)S(1)} %get-tuple-element.41), channel_id=1, source_target_pairs={{0,1},{1,2},{2,3},{4,5},{5,6},{6,7},{8,9},{9,10},{10,11},{12,13},{... | collective-permute-start | bytes 18440 | tf_op jit(solution)/shard_map/ppermute | solution.py:23
  118.7 4.4 %collective-permute-start.14 = (f32[6,1,256]{2,1,0:T(1,128)S(1)}, f32[6,1,256]{2,1,0:T(1,128)S(1)}, u32[]{:S(2)}, u32[]{:S(2)}) collective-permute-start(f32[6,1,256]{2,1,0:T(1,128)S(1)} %get-tuple-element.42), channel_id=1, source_target_pairs={{1,0},{2,1},{3,2},{5,4},{6,5},{7,6},{9,8},{10,9},{11,10},{13,12},{... | collective-permute-start | bytes 18440 | tf_op jit(solution)/shard_map/ppermute | solution.py:25
  128.6 7.8 %collective-permute-start.16 = (f32[3,3,16,512]{3,2,1,0:T(8,128)S(1)}, f32[3,3,16,512]{3,2,1,0:T(8,128)S(1)}, u32[]{:S(2)}, u32[]{:S(2)}) collective-permute-start(f32[3,3,16,512]{3,2,1,0:T(8,128)S(1)} %get-tuple-element.31), channel_id=1, source_target_pairs={{0,4},{4,8},{8,12},{12,16},{16,20},{20,24},{24,28},{1,5},{5,9},{9,... | collective-permute-start | bytes 884744 | tf_op jit(solution)/shard_map/ppermute | solution.py:23
  132.7 10.5 %collective-permute-start.17 = (f32[3,3,16,512]{3,2,1,0:T(8,128)S(1)}, f32[3,3,16,512]{3,2,1,0:T(8,128)S(1)}, u32[]{:S(2)}, u32[]{:S(2)}) collective-permute-start(f32[3,3,16,512]{3,2,1,0:T(8,128)S(1)} %get-tuple-element.32), channel_id=1, source_target_pairs={{4,0},{8,4},{12,8},{16,12},{20,16},{24,20},{28,24},{5,1},{9,5},{13... | collective-permute-start | bytes 884744 | tf_op jit(solution)/shard_map/ppermute | solution.py:25
  143.5 7.5 %collective-permute-start.19 = (f32[3,14,3,512]{3,1,2,0:T(8,128)S(1)}, f32[3,14,3,512]{3,1,2,0:T(8,128)S(1)}, u32[]{:S(2)}, u32[]{:S(2)}) collective-permute-start(f32[3,14,3,512]{3,1,2,0:T(8,128)S(1)} %copy.60), channel_id=1, source_target_pairs={{1,0},{2,1},{3,2},{5,4},{6,5},{7,6},{9,8},{10,9},{11,10},{13,12},{... | collective-permute-start | bytes 774152 | tf_op jit(solution)/shard_map/ppermute | solution.py:25
  144.8 7.6 %collective-permute-start.18 = (f32[3,14,3,512]{3,1,2,0:T(8,128)S(1)}, f32[3,14,3,512]{3,1,2,0:T(8,128)S(1)}, u32[]{:S(2)}, u32[]{:S(2)}) collective-permute-start(f32[3,14,3,512]{3,1,2,0:T(8,128)S(1)} %copy.59), channel_id=1, source_target_pairs={{0,1},{1,2},{2,3},{4,5},{5,6},{6,7},{8,9},{9,10},{10,11},{12,13},{... | collective-permute-start | bytes 774152 | tf_op jit(solution)/shard_map/ppermute | solution.py:23
where the time goes:
time: 160 us; the launch traced here: 157 us
  starting transfers between devices  54.4 us (34%)
  local copies, waits for them, and re-layouts  42.2 us (26%)
  other arithmetic  29.7 us (19%)
  waiting for transfers between devices  29.1 us (18%)
    ppermute x10, starting transfers between devices, extended(): lax.ppermute(tail, axis, [(i, (i + 1) % count) for i in range(ends)])  38.2 us
    ppermute x10, waiting for transfers between devices, extended(): lax.ppermute(head, axis, [((i + 1) % count, i) for i in range(ends)])  26.1 us
    reshape x1, local copies, waits for them, and re-layouts, per_device(): coefficient.reshape(sx // 2, 2, sy // 2, 2, sz // 2, 2).sum(axis=(1, 3, 5))  18.1 us
    reshape x1, local copies, waits for them, and re-layouts, per_device(): remain.reshape(sx // 2, 2, sy // 2, 2, sz // 2, 2).sum(axis=(1, 3, 5))  18.1 us
    ppermute x10, starting transfers between devices, extended(): lax.ppermute(head, axis, [((i + 1) % count, i) for i in range(ends)])  16.2 us
    reduce_sum x1, other arithmetic, per_device(): coefficient.reshape(sx // 2, 2, sy // 2, 2, sz // 2, 2).sum(axis=(1, 3, 5))  7.59 us
    reduce_sum x1, other arithmetic, per_device(): remain.reshape(sx // 2, 2, sy // 2, 2, sz // 2, 2).sum(axis=(1, 3, 5))  6.99 us
    mul x7, other arithmetic, local_op(): return mask * (coef_ext * laplace(jnp.pad(coef_ext * value, 1)))  4.13 us
  transfers between devices with their start and end apart: 20, of which 10 were waited for; matrix products, arithmetic and copies ran while one was open for 18% of the time, Pallas kernels for 0%

commit v1 on v0

v1 whole, which is shorter than its diff:
```python
import functools

import jax
import jax.numpy as jnp
from jax import lax
from jax.experimental import pallas as pl
from jax.experimental.pallas import tpu as pltpu
from jax.sharding import PartitionSpec as P

CPRE = 3
CPOST = 2
CCOARSE = 4
theta = 1.15
delta = 0.85

ROW = 8
MU = CPRE + 1
MG = CPRE
MS = CPOST
MK = CPOST + 1
MC = (MK + 1) // 2
MR = CCOARSE - 1 + MC
XF = MU
XC = MR

AROUND = ((1, 0), (-1, 0), (0, 1), (0, -1), (1, 1), (1, -1), (-1, 1), (-1, -1))
FAR = ((2, 0), (-2, 0))
MESH = pl.DeviceIdType.MESH


def weights(passes):
    sigma = theta / delta
    rho = 1.0 / sigma
    out = [(0.0, 1.0 / (6.0 * theta))]
    for _ in range(1, passes):
        rho_next = 1.0 / (2.0 * sigma - rho)
        out.append((rho_next * rho, 2.0 * rho_next / delta / 6.0))
        rho = rho_next
    return out


def laplace(ref, p):
    center = ref[p]
    rows, depth = center.shape
    lane = lax.broadcasted_iota(jnp.int32, center.shape, 1)
    beside = ref[p - 1] + ref[p + 1]
    beside = beside + pltpu.roll(center, 1, 0) + pltpu.roll(center, rows - 1, 0)
    below = jnp.where(lane == 0, 0.0, pltpu.roll(center, 1, 1))
    above = jnp.where(lane == depth - 1, 0.0, pltpu.roll(center, depth - 1, 1))
    return 6.0 * center - (beside + below + above)


def kernel(
    forcing_hbm, coef_hbm, guess_hbm, pressure_ref, residual_ref,
    forcing, coef, guess, inv, state, u_ext, g_ext, k_ext, s_ext, r_ext, ea, eb,
    c_ext, sc, ca, cb, cu, fold, spread, in_sem, send_sem, recv_sem,
):
    nx, ny, nz = forcing.shape
    cx, cy, cz = nx // 2, ny // 2, nz // 2
    ix, iy = lax.axis_index("gx"), lax.axis_index("gy")
    px, py = lax.axis_size("gx"), lax.axis_size("gy")
    rows = ny + 2 * ROW
    crows = cy + 2 * ROW

    def exists(dx, dy):
        return (ix + dx >= 0) & (ix + dx < px) & (iy + dy >= 0) & (iy + dy < py)

    loads = [
        pltpu.make_async_copy(src, dst, in_sem.at[i])
        for i, (src, dst) in enumerate(
            ((coef_hbm, coef), (guess_hbm, guess), (forcing_hbm, forcing))
        )
    ]
    for load in loads:
        load.start()

    barrier = pltpu.get_barrier_semaphore()
    for dx, dy in AROUND + FAR:
        @pl.when(exists(dx, dy))
        def _():
            pl.semaphore_signal(barrier, inc=1, device_id=(ix + dx, iy + dy), device_id_type=MESH)

    def span(step, depth, first, count):
        if step == 0:
            return pl.ds(first, count), pl.ds(first, count)
        if step > 0:
            return pl.ds(first + count - depth, depth), pl.ds(first - depth, depth)
        return pl.ds(first, depth), pl.ds(first + count, depth)

    class Margin:
        def __init__(self, ref, base, depth, corner, first, count, tall):
            self.ref, self.base = ref, base
            self.depth, self.corner = depth, corner
            self.first, self.count, self.tall = first, count, tall
            self.dirs = AROUND

        def copy(self, i):
            dx, dy = self.dirs[i]
            if abs(dx) == 2:
                over = self.depth - self.count
                if dx > 0:
                    xs = pl.ds(self.first + self.count - over, over)
                    xd = pl.ds(self.first - self.depth, over)
                else:
                    xs = pl.ds(self.first, over)
                    xd = pl.ds(self.first + self.count + self.depth - over, over)
            else:
                deep = self.corner if dy != 0 else self.depth
                xs, xd = span(dx, min(deep, self.count), self.first, self.count)
            ys, yd = span(dy, ROW, ROW, self.tall)
            return pltpu.make_async_remote_copy(
                src_ref=self.ref.at[xs, ys, :],
                dst_ref=self.ref.at[xd, yd, :],
                send_sem=send_sem.at[self.base + i],
                recv_sem=recv_sem.at[self.base + i],
                device_id=(ix + dx, iy + dy),
                device_id_type=MESH,
            )

        def start(self):
            for i, (dx, dy) in enumerate(self.dirs):
                @pl.when(exists(dx, dy))
                def _():
                    self.copy(i).start()

        def arrive(self):
            for i, (dx, dy) in enumerate(self.dirs):
                @pl.when(exists(-dx, -dy))
                def _():
                    self.copy(i).wait_recv()

        def sent(self):
            for i, (dx, dy) in enumerate(self.dirs):
                @pl.when(exists(dx, dy))
                def _():
                    self.copy(i).wait_send()

    mu = Margin(u_ext, 0, MU, MU - 1, XF, nx, ny)
    mg = Margin(g_ext, 8, MG, MG - 1, XF, nx, ny)
    mk = Margin(k_ext, 16, MK, MK - 1, XF, nx, ny)
    ms = Margin(r_ext, 24, MS, MS - 1, XF, nx, ny)
    mc = Margin(c_ext, 32, MR, MR - 1, XC, cx, cy)
    mc.dirs = AROUND + FAR
    own = pl.ds(ROW, ny)
    cown = pl.ds(ROW, cy)

    def inside(p, first, count, tall, shape):
        glob = ix * count - first + p
        ok = (glob >= 0) & (glob < px * count)
        row = lax.broadcasted_iota(jnp.int32, shape, 0) + (iy * tall - ROW)
        low = jnp.where(ok, 0, py * tall)
        return (row >= low) & (row < py * tall)

    def planes(low, high, body):
        def step(p, carry):
            body(p)
            return carry
        lax.fori_loop(low, high, step, 0)

    loads[0].wait()
    loads[1].wait()
    loads[2].wait()

    def scale(p):
        c = coef[p]
        q = 1.0 / c
        inv[p] = q
        u = c * guess[p]
        u_ext[p + XF, own, :] = u
        state[p] = u
        g_ext[p + XF, own, :] = forcing[p] * q

    planes(0, nx, scale)
    peers = sum(jnp.where(exists(dx, dy), 1, 0) for dx, dy in AROUND + FAR)
    pl.semaphore_wait(barrier, peers)
    mu.start()
    mg.start()

    blocks = nz // 128
    take = (
        lax.broadcasted_iota(jnp.int32, (256, 128), 0) // 2
        == lax.broadcasted_iota(jnp.int32, (256, 128), 1)
    ).astype(jnp.float32)
    give = (
        lax.broadcasted_iota(jnp.int32, (128, 256), 1) // 2
        == lax.broadcasted_iota(jnp.int32, (128, 256), 0)
    ).astype(jnp.float32)
    exact = functools.partial(
        jnp.dot, precision=lax.Precision.HIGHEST, preferred_element_type=jnp.float32
    )

    def folded():
        out = []
        for b in range(0, blocks, 2):
            pair = [
                fold[b + i, pl.ds(0, cx * cy, stride=2), :]
                + fold[b + i, pl.ds(1, cx * cy, stride=2), :]
                for i in range(2)
            ]
            out.append(exact(jnp.concatenate(pair, axis=1), take))
        return jnp.concatenate(out, axis=1)

    def fill(value):
        for q in range(cx):
            total = value(2 * q) + value(2 * q + 1)
            for b in range(blocks):
                fold[b, pl.ds(q * ny, ny), :] = total[:, b * 128 : (b + 1) * 128]

    fill(lambda p: coef[p])
    coarse_inv = 1.0 / (folded() * 0.125)
    sc[...] = coarse_inv * 0.25

    for b in range(blocks // 2):
        wide = exact(coarse_inv[:, b * 128 : (b + 1) * 128], give)
        for i in range(2):
            piece = wide[:, i * 128 : (i + 1) * 128]
            fold[2 * b + i, pl.ds(0, cx * cy, stride=2), :] = piece
            fold[2 * b + i, pl.ds(1, cx * cy, stride=2), :] = piece
    for p in range(nx):
        part = [fold[b, pl.ds((p // 2) * ny, ny), :] for b in range(blocks)]
        k_ext[p + XF, own, :] = coef[p] * jnp.concatenate(part, axis=1)
    mk.start()

    mu.arrive()
    mg.arrive()

    shape = (rows, nz)
    pre = weights(CPRE)
    end = XF + nx
    mask_of = lambda p: inside(p, XF, nx, ny, shape)

    mu.sent()

    def clean(p):
        u_ext[p] = jnp.where(mask_of(p), u_ext[p], 0.0)

    planes(XF - MU, XF, clean)
    planes(end, end + MU, clean)
    if True:
        def clean_own(p):
            for at in (0, ROW + ny):
                row = lax.broadcasted_iota(jnp.int32, (ROW, nz), 0) + (iy * ny - ROW + at)
                ok = (row >= 0) & (row < py * ny)
                u_ext[p, pl.ds(at, ROW), :] = jnp.where(ok, u_ext[p, pl.ds(at, ROW), :], 0.0)
        planes(XF, end, clean_own)

    def first(p):
        s = jnp.where(mask_of(p), g_ext[p] - laplace(u_ext, p), 0.0)
        s_ext[p] = s
        ea[p] = pre[0][1] * s

    planes(XF - MG, end + MG, first)
    now, later = ea, eb
    for k in range(1, CPRE):
        wide = CPRE - k

        def pass_on(p, now=now, later=later, k=k):
            s = jnp.where(mask_of(p), s_ext[p] - laplace(now, p), 0.0)
            s_ext[p] = s
            later[p] = pre[k][0] * now[p] + pre[k][1] * s

        planes(XF - wide, end + wide, pass_on)

        def gather(p, now=now):
            state[p] = state[p] + now[p + XF, own, :]

        planes(0, nx, gather)
        now, later = later, now

    def last(p):
        s = s_ext[p] - laplace(now, p)
        s = s[ROW : ROW + ny]
        r_ext[p, own, :] = s
        q = p - XF
        state[q] = state[q] + now[p, own, :]

    planes(XF, end, last)

    fill(lambda p: coef[p] * r_ext[p + XF, own, :])
    rhs = folded() * sc[...]
    for q in range(cx):
        c_ext[q + XC, cown, :] = rhs[q * cy : (q + 1) * cy]
    mc.start()
    ms.start()
    mc.arrive()
    mc.sent()

    cshape = (crows, cz)
    post = weights(CCOARSE)
    cend = XC + cx
    cmask = lambda p: inside(p, XC, cx, cy, cshape)

    def cfirst(p):
        s = jnp.where(cmask(p), c_ext[p], 0.0)
        c_ext[p] = s
        e = post[0][1] * s
        ca[p] = e
        cu[p] = e

    planes(0, cend + MR, cfirst)
    cnow, clater = ca, cb
    for k in range(1, CCOARSE):
        wide = MR - k

        def cpass(p, cnow=cnow, clater=clater, k=k):
            s = jnp.where(cmask(p), c_ext[p] - laplace(cnow, p), 0.0)
            c_ext[p] = s
            e = post[k][0] * cnow[p] + post[k][1] * s
            clater[p] = e
            cu[p] = cu[p] + e

        planes(XC - wide, cend + wide, cpass)
        cnow, clater = clater, cnow

    cplanes = cx + 2 * MC
    corr = cu[XC - MC : XC - MC + cplanes].reshape(cplanes * crows, cz)
    for b in range(blocks // 2):
        wide = exact(corr[:, b * 128 : (b + 1) * 128], give)
        for i in range(2):
            piece = wide[:, i * 128 : (i + 1) * 128]
            spread[2 * b + i, pl.ds(0, cplanes * crows, stride=2), :] = piece
            spread[2 * b + i, pl.ds(1, cplanes * crows, stride=2), :] = piece
    mk.arrive()
    mk.sent()
    shift = XF - 2 * MC

    def correct(p):
        at = pl.multiple_of(((p - shift) // 2) * (2 * crows) + ROW, ROW)
        part = [spread[b, pl.ds(at, rows), :] for b in range(blocks)]
        w = jnp.where(mask_of(p), k_ext[p] * jnp.concatenate(part, axis=1), 0.0)
        ea[p] = w

    planes(XF - MK, end + MK, correct)
    ms.arrive()
    ms.sent()
    mg.sent()
    after = weights(CPOST)

    def again(p):
        s = jnp.where(mask_of(p), r_ext[p] - laplace(ea, p), 0.0)
        s_ext[p] = s
        eb[p] = after[0][1] * s

    planes(XF - MS, end + MS, again)

    def add(p):
        state[p] = state[p] + ea[p + XF, own, :] + eb[p + XF, own, :]

    planes(0, nx, add)

    def post_pass(p):
        s = jnp.where(mask_of(p), s_ext[p] - laplace(eb, p), 0.0)
        s_ext[p] = s
        ea[p] = after[1][0] * eb[p] + after[1][1] * s

    planes(XF - 1, end + 1, post_pass)

    def finish(p):
        s = s_ext[p] - laplace(ea, p)
        q = p - XF
        residual_ref[q] = s[ROW : ROW + ny] * coef[q]
        pressure_ref[q] = (state[q] + ea[p, own, :]) * inv[q]

    planes(XF, end, finish)


def per_device(forcing, coefficient, guess):
    nx, ny, nz = forcing.shape
    f32 = jnp.float32
    block = pltpu.VMEM((nx, ny, nz), f32)
    fine = pltpu.VMEM((nx + 2 * XF, ny + 2 * ROW, nz), f32)
    cx, cy, cz = nx // 2, ny // 2, nz // 2
    coarse = pltpu.VMEM((cx + 2 * XC, cy + 2 * ROW, cz), f32)
    blocks = nz // 128
    spread_rows = (cx + 2 * MC) * (cy + 2 * ROW) * 2
    return pl.pallas_call(
        kernel,
        name="leg",
        out_shape=[jax.ShapeDtypeStruct((nx, ny, nz), f32)] * 2,
        in_specs=[pl.BlockSpec(memory_space=pl.ANY)] * 3,
        out_specs=[pl.BlockSpec(memory_space=pltpu.VMEM)] * 2,
        scratch_shapes=[block] * 5
        + [fine] * 7
        + [coarse, pltpu.VMEM((cx * cy, cz), f32), coarse, coarse, coarse]
        + [pltpu.VMEM((blocks, cx * ny, 128), f32), pltpu.VMEM((blocks, spread_rows, 128), f32)]
        + [
            pltpu.SemaphoreType.DMA((3,)),
            pltpu.SemaphoreType.DMA((42,)),
            pltpu.SemaphoreType.DMA((42,)),
        ],
        compiler_params=pltpu.CompilerParams(collective_id=0, has_side_effects=True),
    )(forcing, coefficient, guess)


def solution(mesh):
    spec = P("gx", "gy", None)
    return jax.shard_map(
        per_device, mesh=mesh, in_specs=(spec,) * 3, out_specs=(spec,) * 2, check_vma=False
    )
```

time: 160 us -> 38.3 us (0.24); the launches traced: 157 us -> 38.1 us
  starting transfers between devices: 54.4 us -> 0 us
  local copies, waits for them, and re-layouts: 42.2 us -> 2.42 us
  Pallas kernels: 0 us -> 35.1 us
  other arithmetic: 29.7 us -> 0 us
  waiting for transfers between devices: 29.1 us -> 0 us
    ppermute x20 -> x0, starting transfers between devices: 54.4 us -> none  [the longest x10 38.2 us: extended(): lax.ppermute(tail, axis, [(i, (i + 1) % count) for i in range(ends)])]
    reshape x5 -> x0, local copies, waits for them, and re-layouts: 38.2 us -> none  [the longest x1 18.1 us: per_device(): coefficient.reshape(sx // 2, 2, sy // 2, 2, sz // 2, 2).sum(axis=(1, 3, 5))]
    pallas_call x0 -> x1, Pallas kernels: none -> 35.1 us  [per_device(): pl.pallas_call(kernel, name='leg', out_shape=[jax.ShapeDtypeStruct((nx, n...]
    ppermute x20 -> x0, waiting for transfers between devices: 29.1 us -> none  [the longest x10 26.1 us: extended(): lax.ppermute(head, axis, [((i + 1) % count, i) for i in range(ends)])]
    reduce_sum x2 -> x0, other arithmetic: 14.6 us -> none  [the longest x1 7.59 us: per_device(): coefficient.reshape(sx // 2, 2, sy // 2, 2, sz // 2, 2).sum(axis=(1, 3, 5))]
    mul x12 -> x0, other arithmetic: 4.47 us -> none  [the longest x7 4.13 us: local_op(): return mask * (coef_ext * laplace(jnp.pad(coef_ext * value, 1)))]
    another operation x3 -> x0, other arithmetic: 2.83 us -> none  [fine_margin_section(): stacked = jnp.stack((state, forcing, coefficient))]
    div x2 -> x0, other arithmetic: 2.41 us -> none  [chebyshev(): direction = inverse * remain / theta]
  transfers between devices with their start and end apart: 20 -> 0, of which waited for: 10 -> 0; matrix products, arithmetic and copies ran while one was open for 18% -> 0% of each run, Pallas kernels for 0% -> 0%
where the time goes in v1:
time: 38.3 us; the launch traced here: 38.1 us
  Pallas kernels  35.1 us (92%)
  local copies, waits for them, and re-layouts  2.42 us (6%)
  between operations  0.65 us (2%)
    pallas_call x1, Pallas kernels, per_device(): pl.pallas_call(kernel, name='leg', out_shape=[jax.ShapeDtypeStruct((nx, n...  35.1 us
    unnamed x4, local copies, waits for them, and re-layouts  2.42 us

profile of v1, /device:TPU:1, one launch (start us, length us, event | category | flops | bytes accessed | tf_op | source)
XLA Modules:
  0.0 38.1 jit_solution(4824390838047094197)
XLA Ops:
  0.6 35.1 %leg.1 = (f32[8,16,512]{2,1,0:T(8,128)}, f32[8,16,512]{2,1,0:T(8,128)}) custom-call(f32[8,16,512]{2,1,0:T(8,128)} %forcing_hbm.1, f32[8,16,512]{2,1,0:T(8,128)} %coef_hbm.1, f32[8,16,512]{2,1,0:T(8,128)} %guess_hbm.1), custom_call_target="tpu_custom_call" | custom-call | tf_op jit(solution)/shard_map/leg/pallas_call | solution.py:376
  35.7 0.0 copy-start
  35.7 1.7 %copy.7 = f32[8,16,512]{2,1,0:T(8,128)} copy(f32[8,16,512]{2,1,0:T(8,128)} %get-tuple-element.4) | data formatting | bytes 524288
  37.4 0.0 copy-done
  37.4 0.7 %copy.8 = f32[8,16,512]{2,1,0:T(8,128)} copy(f32[8,16,512]{2,1,0:T(8,128)S(1)} %copy-done) | data formatting | bytes 524288
Async XLA Ops:
  35.7 1.7 %copy-start = (f32[8,16,512]{2,1,0:T(8,128)S(1)}, f32[8,16,512]{2,1,0:T(8,128)}, u32[]{:S(2)}) copy-start(f32[8,16,512]{2,1,0:T(8,128)} %get-tuple-element.5) | copy-start | bytes 786436

commit v2 on v1

v2 whole, which is shorter than its diff:
```python
import functools

import jax
import jax.numpy as jnp
from jax import lax
from jax.experimental import pallas as pl
from jax.experimental.pallas import tpu as pltpu
from jax.sharding import PartitionSpec as P

CPRE = 3
CPOST = 2
CCOARSE = 4
theta = 1.15
delta = 0.85

LANES = 128
ROW = 8
MU = CPRE + 1
MG = CPRE
MS = CPOST
MK = CPOST + 1
MC = (MK + 1) // 2
MR = CCOARSE - 1 + MC
CLOW = 1
XF = MU
XC = MR

AROUND = ((1, 0), (-1, 0), (0, 1), (0, -1), (1, 1), (1, -1), (-1, 1), (-1, -1))
FAR = ((2, 0), (-2, 0))
MESH = pl.DeviceIdType.MESH


def weights(passes):
    sigma = theta / delta
    rho = 1.0 / sigma
    out = [(0.0, 1.0 / (6.0 * theta))]
    for _ in range(1, passes):
        rho_next = 1.0 / (2.0 * sigma - rho)
        out.append((rho_next * rho, 2.0 * rho_next / delta / 6.0))
        rho = rho_next
    return out


def laplace(ref, p, low, count, one):
    blocks = ref.shape[1]
    here = pl.ds(low, count)
    center = [ref[p, b, here, :] for b in range(blocks)]
    lane = lax.broadcasted_iota(jnp.int32, center[0].shape, 1)
    first, last = lane == 0, lane == LANES - 1
    up = [pltpu.roll(c, 1, 1) for c in center]
    down = [pltpu.roll(c, LANES - 1, 1) for c in center]
    out = []
    for b in range(blocks):
        below = jnp.where(first, up[b - 1] if b > 0 else 0.0, up[b])
        above = jnp.where(last, down[b + 1] if b + 1 < blocks else 0.0, down[b])
        beside = ref[p - 1, b, here, :] + ref[p + 1, b, here, :]
        along = ref[p, b, pl.ds(low - one, count), :] + ref[p, b, pl.ds(low + one, count), :]
        out.append(6.0 * center[b] - ((beside + along) + (below + above)))
    return out


def kernel(
    forcing_hbm, coef_hbm, guess_hbm, state_out, remain_out,
    forcing, coef, guess, state, u_ext, g_ext, k_ext, s_ext, r_ext, ea, eb,
    packed, landed, c_ext, cs, ca, cb, cu, sc, fold, spread, in_sem, send_sem, recv_sem,
):
    nx, ny, nz = forcing.shape
    cx, cy, cz = nx // 2, ny // 2, nz // 2
    ix, iy = lax.axis_index("gx"), lax.axis_index("gy")
    px, py = lax.axis_size("gx"), lax.axis_size("gy")
    rows = ny + 2 * ROW
    crows = cy + 2 * ROW
    blocks, cblocks = nz // LANES, cz // LANES
    one = jnp.minimum(ix + 1, 1)

    def exists(dx, dy):
        return (ix + dx >= 0) & (ix + dx < px) & (iy + dy >= 0) & (iy + dy < py)

    loads = [
        pltpu.make_async_copy(src, dst, in_sem.at[i])
        for i, (src, dst) in enumerate(
            ((coef_hbm, coef), (guess_hbm, guess), (forcing_hbm, forcing))
        )
    ]
    for load in loads:
        load.start()

    barrier = pltpu.get_barrier_semaphore()
    for dx, dy in AROUND + FAR:
        @pl.when(exists(dx, dy))
        def _():
            pl.semaphore_signal(barrier, inc=1, device_id=(ix + dx, iy + dy), device_id_type=MESH)

    def span(step, depth, first, count):
        if step == 0:
            return pl.ds(first, count), pl.ds(first, count)
        if step > 0:
            return pl.ds(first + count - depth, depth), pl.ds(first - depth, depth)
        return pl.ds(first, depth), pl.ds(first + count, depth)

    used = [0]

    class Copies:
        def __init__(self, items):
            self.items = [(used[0] + i,) + item for i, item in enumerate(items)]
            used[0] += len(items)

        def of(self, item):
            at, dx, dy, src, dst = item
            return pltpu.make_async_remote_copy(
                src_ref=src, dst_ref=dst, send_sem=send_sem.at[at], recv_sem=recv_sem.at[at],
                device_id=(ix + dx, iy + dy), device_id_type=MESH,
            )

        def start(self):
            for item in self.items:
                @pl.when(exists(item[1], item[2]))
                def _():
                    self.of(item).start()

        def arrive(self):
            for item in self.items:
                @pl.when(exists(-item[1], -item[2]))
                def _():
                    self.of(item).wait_recv()

        def sent(self):
            for item in self.items:
                @pl.when(exists(item[1], item[2]))
                def _():
                    self.of(item).wait_send()

    def margin(ref, depth, corner, first, count, tall, dirs):
        items = []
        for dx, dy in dirs:
            if abs(dx) == 2:
                over = depth - count
                if dx > 0:
                    xs, xd = pl.ds(first + count - over, over), pl.ds(first - depth, over)
                else:
                    xs, xd = pl.ds(first, over), pl.ds(first + count + depth - over, over)
            else:
                deep = corner if dy != 0 else depth
                xs, xd = span(dx, min(deep, count), first, count)
            ys, yd = span(dy, ROW, ROW, tall)
            items.append((dx, dy, ref.at[xs, :, ys, :], ref.at[xd, :, yd, :]))
        return items

    items = margin(u_ext, MU, 0, XF, nx, ny, AROUND[:2])
    items += margin(g_ext, MG, 0, XF, nx, ny, AROUND[:2])
    for dx, dy in AROUND[2:]:
        side = 0 if dy > 0 else 1
        xs, xd = span(dx, MU - 1, XF, nx)
        items.append((dx, dy, packed.at[side, xs], landed.at[side, xd]))
    m1 = Copies(items)
    mk = Copies(margin(k_ext, MK, MK - 1, XF, nx, ny, AROUND))
    ms = Copies(margin(r_ext, MS, MS - 1, XF, nx, ny, AROUND))
    mc = Copies(margin(c_ext, MR, MR - 1, XC, cx, cy, AROUND + FAR))
    own = pl.ds(ROW, ny)
    cown = pl.ds(ROW, cy)

    def rowclass(iy_first, count, total):
        row = lax.broadcasted_iota(jnp.int32, (count, LANES), 0) + iy_first
        return jnp.where((row >= 0) & (row < total), 0, 1)

    def plane_in(p, first, count):
        glob = ix * count - first + p
        return jnp.where((glob >= 0) & (glob < px * count), 1, 0)

    def planes(low, high, body, step=2):
        def at(i, carry):
            for j in range(step):
                body(low + i * step + j)
            return carry
        lax.fori_loop(0, (high - low) // step, at, 0)

    lanes = lambda b: slice(b * LANES, (b + 1) * LANES)
    end = XF + nx

    for load in loads:
        load.wait()
    low_half = lax.broadcasted_iota(jnp.int32, (ROW, LANES), 0) < ROW // 2

    def scale(p):
        for b in range(blocks):
            c = coef[p, :, lanes(b)]
            u = c * guess[p, :, lanes(b)]
            g = forcing[p, :, lanes(b)] / c
            u_ext[p + XF, b, own, :] = u
            state[p + XF, b] = u
            g_ext[p + XF, b, own, :] = g
            half = ROW // 2
            packed[0, p + XF, b] = jnp.where(low_half, pltpu.roll(u[ny - ROW :], half, 0), g[ny - ROW :])
            packed[1, p + XF, b] = jnp.where(low_half, u[:ROW], pltpu.roll(g[:ROW], half, 0))

    planes(0, nx, scale)
    peers = sum(jnp.where(exists(dx, dy), 1, 0) for dx, dy in AROUND + FAR)
    pl.semaphore_wait(barrier, peers)
    m1.start()

    take = (
        lax.broadcasted_iota(jnp.int32, (2 * LANES, LANES), 0) // 2
        == lax.broadcasted_iota(jnp.int32, (2 * LANES, LANES), 1)
    ).astype(jnp.float32)
    give = (
        lax.broadcasted_iota(jnp.int32, (LANES, 2 * LANES), 1) // 2
        == lax.broadcasted_iota(jnp.int32, (LANES, 2 * LANES), 0)
    ).astype(jnp.float32)
    exact = functools.partial(
        jnp.dot, precision=lax.Precision.HIGHEST, preferred_element_type=jnp.float32
    )

    def folded():
        out = []
        for b in range(0, blocks, 2):
            pair = [
                fold[b + i, pl.ds(0, cx * cy, stride=2), :]
                + fold[b + i, pl.ds(1, cx * cy, stride=2), :]
                for i in range(2)
            ]
            out.append(exact(jnp.concatenate(pair, axis=1), take))
        return out

    def fill(value):
        for q in range(cx):
            for b in range(blocks):
                fold[b, pl.ds(q * ny, ny), :] = value(2 * q, b) + value(2 * q + 1, b)

    def widen(pieces, ref, count):
        for b, piece in enumerate(pieces):
            wide = exact(piece, give)
            for i in range(2):
                ref[2 * b + i, pl.ds(0, count, stride=2), :] = wide[:, lanes(i)]
                ref[2 * b + i, pl.ds(1, count, stride=2), :] = wide[:, lanes(i)]

    fill(lambda p, b: coef[p, :, lanes(b)])
    inverse = [1.0 / (c * 0.125) for c in folded()]
    for b in range(cblocks):
        sc[b] = inverse[b] * 0.25
    widen(inverse, fold, cx * cy)
    for p in range(nx):
        for b in range(blocks):
            k_ext[p + XF, b, own, :] = coef[p, :, lanes(b)] * fold[b, pl.ds((p // 2) * ny, ny), :]
    mk.start()

    zero = jnp.zeros((ny, LANES), jnp.float32)
    for dx, at in ((-1, 0), (1, end)):
        @pl.when(jnp.logical_not(exists(dx, 0)))
        def _():
            for p in range(MU):
                for b in range(blocks):
                    u_ext[at + p, b, own, :] = zero
    m1.arrive()

    def unpack(p):
        inside = plane_in(p, XF, nx) > 0
        over = inside & exists(0, -1)
        under = inside & exists(0, 1)
        for b in range(blocks):
            a = landed[0, p, b]
            u_ext[p, b, pl.ds(0, ROW), :] = jnp.where(over, pltpu.roll(a, ROW // 2, 0), 0.0)
            g_ext[p, b, pl.ds(0, ROW), :] = a
            a = landed[1, p, b]
            u_ext[p, b, pl.ds(ny + ROW, ROW), :] = jnp.where(under, a, 0.0)
            g_ext[p, b, pl.ds(ny + ROW, ROW), :] = pltpu.roll(a, ROW // 2, 0)

    planes(0, end + XF, unpack)

    low, count = ROW // 2, ny + ROW
    here = pl.ds(low, count)
    kinds = rowclass(iy * ny - ROW + low, count, py * ny)
    pre = weights(CPRE)

    def masked(p, value):
        return jnp.where(kinds < plane_in(p, XF, nx), value, 0.0)

    def first(p):
        for b, lap in enumerate(laplace(u_ext, p, low, count, one)):
            s = masked(p, g_ext[p, b, here, :] - lap)
            s_ext[p, b, here, :] = s
            ea[p, b, here, :] = pre[0][1] * s

    planes(XF - MG, end + MG, first)
    now, later = ea, eb
    for k in range(1, CPRE):
        wide = CPRE - k

        def pass_on(p, now=now, later=later, k=k):
            for b, lap in enumerate(laplace(now, p, low, count, one)):
                s = masked(p, s_ext[p, b, here, :] - lap)
                s_ext[p, b, here, :] = s
                later[p, b, here, :] = pre[k][0] * now[p, b, here, :] + pre[k][1] * s
                state[p, b] = state[p, b] + now[p, b, own, :]

        planes(XF - wide, end + wide, pass_on)
        now, later = later, now

    def last(p):
        for b, lap in enumerate(laplace(now, p, ROW, ny, one)):
            r_ext[p, b, own, :] = s_ext[p, b, own, :] - lap
            state[p, b] = state[p, b] + now[p, b, own, :]

    planes(XF, end, last)

    fill(lambda p, b: coef[p, :, lanes(b)] * r_ext[p + XF, b, own, :])
    for b, rhs in enumerate(folded()):
        rhs = rhs * sc[b]
        for q in range(cx):
            c_ext[q + XC, b, cown, :] = rhs[q * cy : (q + 1) * cy]
    mc.start()
    ms.start()
    mc.arrive()

    clow, ccount = CLOW, crows - 2 * CLOW
    every = pl.ds(clow, ccount)
    post = weights(CCOARSE)
    cend = XC + cx
    ckinds = rowclass(iy * cy - ROW + clow, ccount, py * cy)

    def cmasked(p, value):
        return jnp.where(ckinds < plane_in(p, XC, cx), value, 0.0)

    def cfirst(p):
        for b in range(cblocks):
            s = cmasked(p, c_ext[p, b, every, :])
            cs[p, b, every, :] = s
            e = post[0][1] * s
            ca[p, b, every, :] = e
            cu[p, b, every, :] = e

    planes(0, cend + MR, cfirst)
    cnow, clater = ca, cb
    for k in range(1, CCOARSE):
        wide = MR - k

        def cpass(p, cnow=cnow, clater=clater, k=k):
            for b, lap in enumerate(laplace(cnow, p, clow, ccount, one)):
                s = cmasked(p, cs[p, b, every, :] - lap)
                cs[p, b, every, :] = s
                e = post[k][0] * cnow[p, b, every, :] + post[k][1] * s
                clater[p, b, every, :] = e
                cu[p, b, every, :] = cu[p, b, every, :] + e

        planes(XC - wide, cend + wide, cpass)
        cnow, clater = clater, cnow

    cplanes = cx + 2 * MC
    widen(
        [cu[XC - MC : XC - MC + cplanes, b].reshape(cplanes * crows, LANES) for b in range(cblocks)],
        spread, cplanes * crows,
    )
    mk.arrive()
    shift = XF - 2 * MC

    def correct(p):
        at = pl.multiple_of(((p - shift) // 2) * (2 * crows) + ROW, ROW)
        for b in range(blocks):
            w = k_ext[p, b, here, :] * spread[b, pl.ds(at + low, count), :]
            ea[p, b, here, :] = masked(p, w)

    planes(XF - MK, end + MK, correct)
    ms.arrive()
    after = weights(CPOST)

    def again(p):
        for b, lap in enumerate(laplace(ea, p, low, count, one)):
            s = masked(p, r_ext[p, b, here, :] - lap)
            s_ext[p, b, here, :] = s
            eb[p, b, here, :] = after[0][1] * s

    planes(XF - MS, end + MS, again)

    def post_pass(p):
        for b, lap in enumerate(laplace(eb, p, low, count, one)):
            s = masked(p, s_ext[p, b, here, :] - lap)
            s_ext[p, b, here, :] = s
            e = after[1][0] * eb[p, b, here, :] + after[1][1] * s
            state[p, b] = state[p, b] + ea[p, b, own, :] + eb[p, b, own, :]
            ea[p, b, here, :] = e

    planes(XF - 1, end + 1, post_pass)

    def finish(p):
        for b, lap in enumerate(laplace(ea, p, ROW, ny, one)):
            remain_out[p - XF, :, lanes(b)] = s_ext[p, b, own, :] - lap
            state_out[p - XF, :, lanes(b)] = state[p, b] + ea[p, b, own, :]

    planes(XF, end, finish)
    for copies in (m1, mk, ms, mc):
        copies.sent()


def per_device(forcing, coefficient, guess):
    nx, ny, nz = forcing.shape
    f32 = jnp.float32
    blocks = nz // LANES
    block = pltpu.VMEM((nx, ny, nz), f32)
    fine = pltpu.VMEM((nx + 2 * XF, blocks, ny + 2 * ROW, LANES), f32)
    kept = pltpu.VMEM((nx + 2 * XF, blocks, ny, LANES), f32)
    edge = pltpu.VMEM((2, nx + 2 * XF, blocks, ROW, LANES), f32)
    cx, cy = nx // 2, ny // 2
    coarse = pltpu.VMEM((cx + 2 * XC, blocks // 2, cy + 2 * ROW, LANES), f32)
    spread_rows = (cx + 2 * MC) * (cy + 2 * ROW) * 2
    state, remain = pl.pallas_call(
        kernel,
        name="leg",
        out_shape=[jax.ShapeDtypeStruct((nx, ny, nz), f32)] * 2,
        in_specs=[pl.BlockSpec(memory_space=pl.ANY)] * 3,
        out_specs=[pl.BlockSpec(memory_space=pltpu.VMEM)] * 2,
        scratch_shapes=[block] * 3
        + [kept]
        + [fine] * 7
        + [edge] * 2
        + [coarse] * 5
        + [pltpu.VMEM((blocks // 2, cx * cy, LANES), f32)]
        + [pltpu.VMEM((blocks, cx * ny, LANES), f32), pltpu.VMEM((blocks, spread_rows, LANES), f32)]
        + [
            pltpu.SemaphoreType.DMA((3,)),
            pltpu.SemaphoreType.DMA((36,)),
            pltpu.SemaphoreType.DMA((36,)),
        ],
        compiler_params=pltpu.CompilerParams(collective_id=0, has_side_effects=True),
    )(forcing, coefficient, guess)
    return state / coefficient, remain * coefficient


def solution(mesh):
    spec = P("gx", "gy", None)
    return jax.shard_map(
        per_device, mesh=mesh, in_specs=(spec,) * 3, out_specs=(spec,) * 2, check_vma=False
    )
```

time: 38.3 us -> 29.7 us (0.78)
  the two profiles are of different devices: /device:TPU:1 before, /device:TPU:3 now
where the time goes in v2:
time: 29.7 us; the launch traced here: 29.5 us
  Pallas kernels  27 us (91%)
  other arithmetic  1.88 us (6%)
  between operations  0.65 us (2%)
    pallas_call x1, Pallas kernels, per_device(): pl.pallas_call(kernel, name='leg', out_shape=[jax.ShapeDtypeStruct((nx, n...  27 us
    mul x1, other arithmetic, per_device(): return (state / coefficient, remain * coefficient)  1.88 us

profile of v2, /device:TPU:3, one launch (start us, length us, event | category | flops | bytes accessed | tf_op | source)
XLA Modules:
  0.0 29.5 jit_solution(15663447056539338211)
XLA Ops:
  0.6 0.0 copy-start
  0.6 27.0 %leg.1 = (f32[8,16,512]{2,1,0:T(8,128)}, f32[8,16,512]{2,1,0:T(8,128)}) custom-call(f32[8,16,512]{2,1,0:T(8,128)} %forcing_hbm.1, f32[8,16,512]{2,1,0:T(8,128)} %coef_hbm.1, f32[8,16,512]{2,1,0:T(8,128)} %guess_hbm.1), custom_call_target="tpu_custom_call" | custom-call | tf_op jit(solution)/shard_map/leg/pallas_call | solution.py:404
  27.6 0.0 copy-done
  27.6 1.9 %fusion = (f32[8,16,512]{2,1,0:T(8,128)}, f32[8,16,512]{2,1,0:T(8,128)}) fusion(f32[8,16,512]{2,1,0:T(8,128)} %get-tuple-element.5, f32[8,16,512]{2,1,0:T(8,128)S(1)} %copy-done, f32[8,16,512]{2,1,0:T(8,128)} %get-tuple-element.4), kind=kLoop, calls=%fused_computation | loop fusion | flops 131072 | bytes 1310720 | tf_op jit(solution)/shard_map/mul | solution.py:424
Async XLA Ops:
  0.6 27.0 %copy-start = (f32[8,16,512]{2,1,0:T(8,128)S(1)}, f32[8,16,512]{2,1,0:T(8,128)}, u32[]{:S(2)}) copy-start(f32[8,16,512]{2,1,0:T(8,128)} %coef_hbm.1) | copy-start | bytes 786436

commit v3 on v2

--- a/solution.py
+++ b/solution.py
@@ -14,6 +14,8 @@
 delta = 0.85
 
 LANES = 128
+STEP = 14
+WHOLE = 14
 ROW = 8
 MU = CPRE + 1
 MG = CPRE
@@ -61,7 +63,7 @@
 
 def kernel(
     forcing_hbm, coef_hbm, guess_hbm, state_out, remain_out,
-    forcing, coef, guess, state, u_ext, g_ext, k_ext, s_ext, r_ext, ea, eb,
+    forcing, coef, guess, state, u_ext, g_ext, k_ext, s_ext, r_ext, ea, eb, ec,
     packed, landed, c_ext, cs, ca, cb, cu, sc, fold, spread, in_sem, send_sem, recv_sem,
 ):
     nx, ny, nz = forcing.shape
@@ -146,16 +148,23 @@
             items.append((dx, dy, ref.at[xs, :, ys, :], ref.at[xd, :, yd, :]))
         return items
 
-    items = margin(u_ext, MU, 0, XF, nx, ny, AROUND[:2])
-    items += margin(g_ext, MG, 0, XF, nx, ny, AROUND[:2])
-    for dx, dy in AROUND[2:]:
-        side = 0 if dy > 0 else 1
-        xs, xd = span(dx, MU - 1, XF, nx)
-        items.append((dx, dy, packed.at[side, xs], landed.at[side, xd]))
-    m1 = Copies(items)
+    def beside(dirs):
+        items = []
+        for dx, dy in dirs:
+            side = 0 if dy > 0 else 1
+            xs, xd = span(dx, MU - 1, XF, nx)
+            items.append((dx, dy, packed.at[side, xs], landed.at[side, xd]))
+        return items
+
+    my = Copies(beside(AROUND[2:4]))
+    m1 = Copies(
+        margin(u_ext, MU, 0, XF, nx, ny, AROUND[:2])
+        + margin(g_ext, MG, 0, XF, nx, ny, AROUND[:2])
+        + beside(AROUND[4:])
+    )
     mk = Copies(margin(k_ext, MK, MK - 1, XF, nx, ny, AROUND))
     ms = Copies(margin(r_ext, MS, MS - 1, XF, nx, ny, AROUND))
-    mc = Copies(margin(c_ext, MR, MR - 1, XC, cx, cy, AROUND + FAR))
+    mc = Copies(margin(c_ext, MR, MR - 1, XC, cx, cy, FAR + AROUND[4:] + AROUND[:4]))
     own = pl.ds(ROW, ny)
     cown = pl.ds(ROW, cy)
 
@@ -167,7 +176,11 @@
         glob = ix * count - first + p
         return jnp.where((glob >= 0) & (glob < px * count), 1, 0)
 
-    def planes(low, high, body, step=2):
+    def planes(low, high, body, step=STEP):
+        if high <= low:
+            return
+        step = next(n for n in range(step, 0, -1) if (high - low) % n == 0)
+
         def at(i, carry):
             for j in range(step):
                 body(low + i * step + j)
@@ -196,6 +209,7 @@
     planes(0, nx, scale)
     peers = sum(jnp.where(exists(dx, dy), 1, 0) for dx, dy in AROUND + FAR)
     pl.semaphore_wait(barrier, peers)
+    my.start()
     m1.start()
 
     take = (
@@ -250,8 +264,6 @@
             for p in range(MU):
                 for b in range(blocks):
                     u_ext[at + p, b, own, :] = zero
-    m1.arrive()
-
     def unpack(p):
         inside = plane_in(p, XF, nx) > 0
         over = inside & exists(0, -1)
@@ -264,8 +276,6 @@
             u_ext[p, b, pl.ds(ny + ROW, ROW), :] = jnp.where(under, a, 0.0)
             g_ext[p, b, pl.ds(ny + ROW, ROW), :] = pltpu.roll(a, ROW // 2, 0)
 
-    planes(0, end + XF, unpack)
-
     low, count = ROW // 2, ny + ROW
     here = pl.ds(low, count)
     kinds = rowclass(iy * ny - ROW + low, count, py * ny)
@@ -280,20 +290,32 @@
             s_ext[p, b, here, :] = s
             ea[p, b, here, :] = pre[0][1] * s
 
-    planes(XF - MG, end + MG, first)
-    now, later = ea, eb
-    for k in range(1, CPRE):
-        wide = CPRE - k
-
-        def pass_on(p, now=now, later=later, k=k):
+    def pass_of(k):
+        now, later = steps[k - 1], steps[k]
+
+        def pass_on(p):
             for b, lap in enumerate(laplace(now, p, low, count, one)):
                 s = masked(p, s_ext[p, b, here, :] - lap)
                 s_ext[p, b, here, :] = s
                 later[p, b, here, :] = pre[k][0] * now[p, b, here, :] + pre[k][1] * s
                 state[p, b] = state[p, b] + now[p, b, own, :]
 
-        planes(XF - wide, end + wide, pass_on)
-        now, later = later, now
+        return pass_on
+
+    steps = (ea, eb, ec)
+    stages = [first] + [pass_of(k) for k in range(1, CPRE)]
+    inner = lambda k: min(k + 1, nx // 2)
+    my.arrive()
+    planes(XF, end, unpack)
+    for k, stage in enumerate(stages):
+        planes(XF + inner(k), end - inner(k), stage)
+    m1.arrive()
+    planes(0, XF, unpack)
+    planes(end, end + XF, unpack)
+    for k, stage in enumerate(stages):
+        planes(XF - (CPRE - k), XF + inner(k), stage)
+        planes(end - inner(k), end + (CPRE - k), stage)
+    now = steps[CPRE - 1]
 
     def last(p):
         for b, lap in enumerate(laplace(now, p, ROW, ny, one)):
@@ -328,7 +350,7 @@
             ca[p, b, every, :] = e
             cu[p, b, every, :] = e
 
-    planes(0, cend + MR, cfirst)
+    planes(0, cend + MR, cfirst, WHOLE)
     cnow, clater = ca, cb
     for k in range(1, CCOARSE):
         wide = MR - k
@@ -341,7 +363,7 @@
                 clater[p, b, every, :] = e
                 cu[p, b, every, :] = cu[p, b, every, :] + e
 
-        planes(XC - wide, cend + wide, cpass)
+        planes(XC - wide, cend + wide, cpass, WHOLE)
         cnow, clater = clater, cnow
 
     cplanes = cx + 2 * MC
@@ -386,7 +408,7 @@
             state_out[p - XF, :, lanes(b)] = state[p, b] + ea[p, b, own, :]
 
     planes(XF, end, finish)
-    for copies in (m1, mk, ms, mc):
+    for copies in (my, m1, mk, ms, mc):
         copies.sent()
 
 
@@ -409,7 +431,7 @@
         out_specs=[pl.BlockSpec(memory_space=pltpu.VMEM)] * 2,
         scratch_shapes=[block] * 3
         + [kept]
-        + [fine] * 7
+        + [fine] * 8
         + [edge] * 2
         + [coarse] * 5
         + [pltpu.VMEM((blocks // 2, cx * cy, LANES), f32)]

time: 29.7 us -> 26.4 us (0.89)
  the two profiles are of different devices: /device:TPU:3 before, /device:TPU:1 now
where the time goes in v3:
time: 26.4 us; the launch traced here: 26 us
  Pallas kernels  23.4 us (89%)
  other arithmetic  1.88 us (7%)
  between operations  0.65 us (2%)
    pallas_call x1, Pallas kernels, per_device(): pl.pallas_call(kernel, name='leg', out_shape=[jax.ShapeDtypeStruct((nx, n...  23.4 us
    mul x1, other arithmetic, per_device(): return (state / coefficient, remain * coefficient)  1.88 us

profile of v3, /device:TPU:1, one launch (start us, length us, event | category | flops | bytes accessed | tf_op | source)
XLA Modules:
  0.0 26.0 jit_solution(9800710885071905035)
XLA Ops:
  0.6 0.0 copy-start
  0.6 23.4 %leg.1 = (f32[8,16,512]{2,1,0:T(8,128)}, f32[8,16,512]{2,1,0:T(8,128)}) custom-call(f32[8,16,512]{2,1,0:T(8,128)} %forcing_hbm.1, f32[8,16,512]{2,1,0:T(8,128)} %coef_hbm.1, f32[8,16,512]{2,1,0:T(8,128)} %guess_hbm.1), custom_call_target="tpu_custom_call" | custom-call | tf_op jit(solution)/shard_map/leg/pallas_call | solution.py:426
  24.1 0.0 copy-done
  24.1 1.9 %fusion = (f32[8,16,512]{2,1,0:T(8,128)}, f32[8,16,512]{2,1,0:T(8,128)}) fusion(f32[8,16,512]{2,1,0:T(8,128)} %get-tuple-element.5, f32[8,16,512]{2,1,0:T(8,128)S(1)} %copy-done, f32[8,16,512]{2,1,0:T(8,128)} %get-tuple-element.4), kind=kLoop, calls=%fused_computation | loop fusion | flops 131072 | bytes 1310720 | tf_op jit(solution)/shard_map/mul | solution.py:446
Async XLA Ops:
  0.6 23.5 %copy-start = (f32[8,16,512]{2,1,0:T(8,128)S(1)}, f32[8,16,512]{2,1,0:T(8,128)}, u32[]{:S(2)}) copy-start(f32[8,16,512]{2,1,0:T(8,128)} %coef_hbm.1) | copy-start | bytes 786436
